TPU v7x, 32 devices: a whole 2x2x4 slice. The times are simulated.
32 devices in a mesh: los: 8 (over z, x), sky: 4 (over y, core).
Axes of the slice: x: 2, y: 2, z: 4, core: 2. Of those that a mesh axis runs over, the one named last changes fastest.
Arguments:
- potentials: bfloat16 [32, 64, 4096], P('los', 'sky'), may hold values from -6 to 6
- shell_weight: float32 [32], P('los'), may hold values from 0.004 to 0.02
- shell_dist: float32 [32], P('los'), may hold values from 1 to 2.28, as said below
- source_dist: float32 [32], P('los'), may hold values from 1 to 2.28, as said below
Outputs:
- convergence: bfloat16 [32, 64, 4096], P('los', 'sky')
- shear_one: bfloat16 [32, 64, 4096], P('los', 'sky')
- shear_two: bfloat16 [32, 64, 4096], P('los', 'sky')
Inputs may be any that keep to these rules, and one draw needn't show every extreme that they name: shell_dist rises strictly with the shell index. source_dist[s] lies strictly between shell_dist[s] and shell_dist[s + 1].
All inputs are finite; a program needn't handle non-finite values.
Results may differ from a plain program's by a relative error of at most 0.001.
Values may be sent and summed in bfloat16 or wider, within the bound.
A program may use at most 64 MiB of HBM per device.

v0:
```python
import functools

import jax
import jax.numpy as jnp
from jax import lax
from jax.experimental import pallas as pl
from jax.experimental.pallas import tpu as pltpu
from jax.sharding import PartitionSpec as P

MESH = pl.DeviceIdType.MESH


def lens_kernel(
    los, sky, chunks, width, weight_ref, dist_ref, source_ref, pot_hbm,
    conv_ref, one_ref, two_ref,
    pot, edge_send, edge_recv, sent, own, got, sent_rim, own_rim, got_rim,
    before, before_rim, onward, onward_rim, back, back_rim,
    prefix, prefix_rim, rim_pot, lens,
    load_sem, edge_ssem, edge_rsem, x_ssem, x_rsem, z_ssem, z_rsem, b_ssem, b_rsem,
):
    f32 = jnp.float32
    shells, rows = pot.shape[0], pot.shape[1]
    half = chunks * width
    me = lax.axis_index("los")
    strip = lax.axis_index("sky")
    q = me // 2
    r = me % 2
    last = los // 2 - 1
    partner = me + 1 - 2 * r
    up = (strip + sky - 1) % sky
    down = (strip + 1) % sky

    span = 2 * chunks
    loads = []
    for c in range(span):
        part = (1 - r) if c < chunks else r
        cols = pl.ds(pl.multiple_of((part * chunks + c % chunks) * width, 128), width)
        loads.append(
            pltpu.make_async_copy(pot_hbm.at[:, :, cols], pot.at[:, :, cols], load_sem.at[c])
        )
        loads[-1].start()

    barrier = pltpu.get_barrier_semaphore()
    pl.semaphore_signal(barrier, inc=1, device_id={"los": partner}, device_id_type=MESH)
    pl.semaphore_signal(barrier, inc=1, device_id={"sky": up}, device_id_type=MESH)
    pl.semaphore_signal(barrier, inc=1, device_id={"sky": down}, device_id_type=MESH)

    @pl.when(q > 0)
    def _():
        pl.semaphore_signal(barrier, inc=1, device_id={"los": me - 2}, device_id_type=MESH)

    @pl.when(q < last)
    def _():
        pl.semaphore_signal(barrier, inc=1, device_id={"los": me + 2}, device_id_type=MESH)

    near = [weight_ref[j] * dist_ref[j] for j in range(shells)]
    far = [near[j] * dist_ref[j] for j in range(shells)]
    row = lax.broadcasted_iota(jnp.int32, (8, width), 0)

    def totals(start):
        cols = pl.ds(pl.multiple_of(start, 128), width)
        total_near = jnp.zeros((rows, width), f32)
        total_far = jnp.zeros((rows, width), f32)
        for j in range(shells):
            block = pot[j, :, cols].astype(f32)
            total_near = total_near + near[j] * block
            total_far = total_far + far[j] * block
        return jnp.concatenate([total_near, total_far], axis=0)

    def remote(src, dst, ssem, rsem, **where):
        return pltpu.make_async_remote_copy(
            src_ref=src, dst_ref=dst, send_sem=ssem, recv_sem=rsem,
            device_id=where, device_id_type=MESH,
        )

    x_copies = [
        remote(sent.at[c], got.at[c], x_ssem.at[c], x_rsem.at[c], los=partner)
        for c in range(chunks)
    ] + [remote(sent_rim, got_rim, x_ssem.at[chunks], x_rsem.at[chunks], los=partner)]
    z_copies = [
        remote(onward.at[c], before.at[c], z_ssem.at[c], z_rsem.at[c], los=me + 2)
        for c in range(chunks)
    ] + [remote(onward_rim, before_rim, z_ssem.at[chunks], z_rsem.at[chunks], los=me + 2)]
    b_copies = [
        remote(back.at[c], prefix.at[r, c], b_ssem.at[c], b_rsem.at[c], los=partner)
        for c in range(chunks)
    ] + [remote(back_rim, prefix_rim.at[r], b_ssem.at[chunks], b_rsem.at[chunks], los=partner)]

    edges = [
        remote(edge_send.at[0], edge_recv.at[0], edge_ssem.at[0], edge_rsem.at[0], sky=up),
        remote(edge_send.at[1], edge_recv.at[1], edge_ssem.at[1], edge_rsem.at[1], sky=down),
    ]
    rim_at = max(1, chunks * 5 // 8)

    def send_totals(c):
        sent[c] = totals((1 - r) * half + c * width)
        x_copies[c].start()

    loads[0].wait()
    sent[0] = totals((1 - r) * half)

    peers = 3 + (q > 0).astype(jnp.int32) + (q < last).astype(jnp.int32)
    pl.semaphore_wait(barrier, peers)

    x_copies[0].start()
    for copy in loads[1:]:
        copy.wait()

    for k in range(span):
        cols = pl.ds(k * width, width)
        top = jnp.zeros((8, width), f32)
        bottom = jnp.zeros((8, width), f32)
        for j in range(shells):
            block = pot[j, :, cols].astype(f32)
            mine = (row >= 2 * j) & (row < 2 * j + 2)
            head = block[:8]
            tail = block[rows - 8 :]
            top = jnp.where(mine, pltpu.roll(head, (2 * j) % 8, 0), top)
            bottom = jnp.where(mine, pltpu.roll(tail, (2 * j + 2) % 8, 0), bottom)
        edge_send[0, :, cols] = top.astype(jnp.bfloat16)
        edge_send[1, :, cols] = bottom.astype(jnp.bfloat16)

    for copy in edges:
        copy.start()
    for c in range(1, rim_at):
        send_totals(c)
    for c in range(chunks):
        own[c] = totals(r * half + c * width)

    @pl.when(q == 0)
    def _():
        before[...] = jnp.zeros(before.shape, f32)
        before_rim[...] = jnp.zeros(before_rim.shape, f32)

    for copy in edges:
        copy.wait_recv()

    inner = (row >= 2) & (row < 6)
    for k in range(span):
        cols = pl.ds(k * width, width)
        below = edge_recv[0, :, cols].astype(f32)
        above = edge_recv[1, :, cols].astype(f32)
        total = jnp.zeros((8, width), f32)
        for j in range(shells):
            tile = jnp.where(
                row < 2,
                pltpu.roll(below, (8 - 2 * j) % 8, 0),
                jnp.where(
                    row < 4,
                    pltpu.roll(below, (10 - 2 * j) % 8, 0),
                    jnp.where(
                        row < 6,
                        pltpu.roll(above, (12 - 2 * j) % 8, 0),
                        pltpu.roll(above, (14 - 2 * j) % 8, 0),
                    ),
                ),
            )
            scaled = tile * jnp.where(inner, far[j], near[j])
            rim_pot[j, k] = scaled
            total = total + scaled
        own_rim[k // chunks, k % chunks] = total
    sent_rim[...] = own_rim[1 - r]
    x_copies[chunks].start()

    for c in range(rim_at, chunks):
        send_totals(c)

    is_odd = r.astype(f32)
    is_even = 1.0 - is_odd

    def forward(c):
        x_copies[c].wait_recv()

        @pl.when(q > 0)
        def _():
            z_copies[c].wait_recv()

        if c < chunks:
            mine, other, base = own[c], got[c], before[c]
            next_ref, back_ref, keep_ref = onward.at[c], back.at[c], prefix.at[r, c]
        else:
            mine, other, base = own_rim[r], got_rim[...], before_rim[...]
            next_ref, back_ref, keep_ref = onward_rim, back_rim, prefix_rim.at[r]
        next_ref[...] = base + (mine + other)

        @pl.when(q < last)
        def _():
            z_copies[c].start()

        back_ref[...] = base + is_even * mine
        b_copies[c].start()
        keep_ref[...] = base + is_odd * other

    inverse = [1.0 / jnp.full((8, width), source_ref[j], f32) for j in range(shells)]

    def lens_chunk(place, carry):
        k = (r * chunks + place) % span
        cols = pl.ds(pl.multiple_of(k * width, 128), width)
        part, c = k // chunks, k % chunks
        sums = prefix[part, c]
        run_near, run_far = sums[:rows], sums[rows:]
        rim = prefix_rim[part, c]
        for j in range(shells):
            block = pot[j, :, cols].astype(f32)
            run_near = run_near + near[j] * block
            run_far = run_far + far[j] * block
            rim = rim + rim_pot[j, k]
            far_rim = jnp.where(row < 4, pltpu.roll(rim, 6, 0), pltpu.roll(rim, 2, 0))
            scale = jnp.concatenate([inverse[j]] * (rows // 8), axis=0)
            lens[j, k, :rows] = run_near - run_far * scale
            lens[j, k, rows:] = rim - far_rim * inverse[j]
        return carry

    def stencil_chunk(place, carry):
        k = (r * chunks + place) % span
        cols = pl.ds(pl.multiple_of(k * width, 128), width)
        before_k = (k + span - 1) % span
        after_k = (k + 1) % span
        for j in range(shells):
            centre = lens[j, k]
            wide = jnp.concatenate(
                [lens[j, before_k, :, width - 128 :], centre, lens[j, after_k, :, :128]], axis=1
            )
            full = width + 256

            def shift(n):
                return pltpu.roll(wide, n % full, 1)[:, 128 : 128 + width]

            left1, right1, left2, right2 = shift(1), shift(-1), shift(2), shift(-2)
            slope = (left2 - right2) + 8.0 * (right1 - left1)
            second_x = (16.0 * (left1 + right1) - (left2 + right2))[:rows]

            def rows_at(field, n):
                return pltpu.roll(field, (-n) % (rows + 8), 0)[:rows]

            second_y = 16.0 * (rows_at(centre, -1) + rows_at(centre, 1)) - (
                rows_at(centre, -2) + rows_at(centre, 2)
            )
            cross = (rows_at(slope, -2) - rows_at(slope, 2)) + 8.0 * (
                rows_at(slope, 1) - rows_at(slope, -1)
            )
            middle = 60.0 * centre[:rows]
            conv_ref[j, :, cols] = ((second_x + second_y - middle) * (1.0 / 24.0)).astype(jnp.bfloat16)
            one_ref[j, :, cols] = ((second_x - second_y) * (1.0 / 24.0)).astype(jnp.bfloat16)
            two_ref[j, :, cols] = (cross * (1.0 / 144.0)).astype(jnp.bfloat16)
        return carry

    order = list(range(rim_at)) + [chunks] + list(range(rim_at, chunks))

    @pl.when(q < last)
    def _():
        for c in order:
            forward(c)
        lax.fori_loop(0, chunks, lens_chunk, 0)
        lax.fori_loop(1, chunks - 1, stencil_chunk, 0)
        for c in order:
            b_copies[c].wait_recv()
        lax.fori_loop(chunks, span, lens_chunk, 0)
        lax.fori_loop(chunks - 1, span + 1, stencil_chunk, 0)

    @pl.when(q == last)
    def _():
        arrived, mapped, done = set(), set(), set()

        def run(body, places):
            while places:
                count = 1
                while count < len(places) and places[count] == places[0] + count:
                    count += 1
                lax.fori_loop(places[0], places[0] + count, body, 0)
                places = places[count:]

        def advance(limit):
            ready = []
            for place in sorted(arrived - mapped):
                rim_place = "own" if place < chunks else "other"
                if rim_place in rims:
                    ready.append(place)
            run(lens_chunk, ready)
            mapped.update(ready)
            ready = [
                place
                for place in range(span)
                if place not in done
                and {(place - 1) % span, place, (place + 1) % span} <= mapped
            ][:limit]
            run(stencil_chunk, ready)
            done.update(ready)

        rims = set()

        def receive(c):
            b_copies[c].wait_recv()
            if c == chunks:
                rims.add("other")
            else:
                arrived.add(chunks + c)

        waited = 0
        for n, c in enumerate(order):
            forward(c)
            if c == chunks:
                rims.add("own")
            else:
                arrived.add(c)
            if "own" in rims and n > rim_at:
                while waited < n - 1:
                    receive(order[waited])
                    waited += 1
            advance(4)
        for c in order[waited:]:
            receive(c)
            advance(span)

    for copy in edges:
        copy.wait_send()
    for c in range(chunks + 1):
        x_copies[c].wait_send()
        b_copies[c].wait_send()

    @pl.when(q < last)
    def _():
        for c in range(chunks + 1):
            z_copies[c].wait_send()


def store_kernel(a, b, c, to_a, to_b, to_c, sems):
    copies = [
        pltpu.make_async_copy(src.at[j], dst.at[j], sems.at[n, j])
        for n, (src, dst) in enumerate(((a, to_a), (b, to_b), (c, to_c)))
        for j in range(a.shape[0])
    ]
    for copy in copies:
        copy.start()
    for copy in copies:
        copy.wait()


def on_device(los, sky, potentials, shell_weight, shell_dist, source_dist):
    shells, rows, ncols = potentials.shape
    half = ncols // 2
    chunks = next(n for n in (4, 2, 1) if half % (n * 128) == 0)
    width = half // chunks
    f32, bf16 = jnp.float32, jnp.bfloat16
    dma = pltpu.SemaphoreType.DMA
    smem = pl.BlockSpec(memory_space=pltpu.SMEM)
    vmem = pl.BlockSpec(memory_space=pltpu.VMEM)
    main = (chunks, 2 * rows, width)
    rim = (chunks, 8, width)
    staged = pl.pallas_call(
        functools.partial(lens_kernel, los, sky, chunks, width),
        out_shape=[pltpu.VMEM(potentials.shape, bf16)] * 3,
        in_specs=[smem, smem, smem, pl.BlockSpec(memory_space=pl.ANY)],
        out_specs=[vmem] * 3,
        scratch_shapes=[
            pltpu.VMEM(potentials.shape, bf16),
            pltpu.VMEM((2, 8, ncols), bf16),
            pltpu.VMEM((2, 8, ncols), bf16),
            pltpu.VMEM(main, f32),
            pltpu.VMEM(main, f32),
            pltpu.VMEM(main, f32),
            pltpu.VMEM(rim, f32),
            pltpu.VMEM((2,) + rim, f32),
            pltpu.VMEM(rim, f32),
            pltpu.VMEM(main, f32),
            pltpu.VMEM(rim, f32),
            pltpu.VMEM(main, f32),
            pltpu.VMEM(rim, f32),
            pltpu.VMEM(main, f32),
            pltpu.VMEM(rim, f32),
            pltpu.VMEM((2,) + main, f32),
            pltpu.VMEM((2,) + rim, f32),
            pltpu.VMEM((shells, 2 * chunks, 8, width), f32),
            pltpu.VMEM((shells, 2 * chunks, rows + 8, width), f32),
            dma((2 * chunks,)),
            dma((2,)),
            dma((2,)),
            dma((chunks + 1,)),
            dma((chunks + 1,)),
            dma((chunks + 1,)),
            dma((chunks + 1,)),
            dma((chunks + 1,)),
            dma((chunks + 1,)),
        ],
        compiler_params=pltpu.CompilerParams(collective_id=0, has_side_effects=True),
    )(shell_weight, shell_dist, source_dist, potentials)
    anywhere = pl.BlockSpec(memory_space=pl.ANY)
    return tuple(pl.pallas_call(
        store_kernel,
        out_shape=[jax.ShapeDtypeStruct(potentials.shape, bf16)] * 3,
        in_specs=[vmem] * 3,
        out_specs=[anywhere] * 3,
        scratch_shapes=[dma((3, shells))],
    )(*[pltpu.with_memory_space_constraint(x, pltpu.VMEM) for x in staged]))


def solution(mesh):
    return jax.shard_map(
        functools.partial(on_device, mesh.shape["los"], mesh.shape["sky"]),
        mesh=mesh,
        in_specs=(P("los", "sky", None), P("los"), P("los"), P("los")),
        out_specs=(P("los", "sky", None), P("los", "sky", None), P("los", "sky", None)),
        check_vma=False,
    )
```

profile of v0, /device:TPU:24, one launch (start us, length us, event | category | flops | bytes accessed | tf_op | source)
XLA Modules:
  0.0 27.7 jit_solution(14961766212421034836)
XLA Ops:
  0.6 25.8 %shard_map.67 = (bf16[4,16,4096]{2,1,0:T(8,128)(2,1)S(1)}, bf16[4,16,4096]{2,1,0:T(8,128)(2,1)S(1)}, bf16[4,16,4096]{2,1,0:T(8,128)(2,1)S(1)}) custom-call(f32[4]{0:T(128)} %weight_ref.1, f32[4]{0:T(128)} %dist_ref.1, f32[4]{0:T(128)} %source_ref.1, bf16[4,16,4096]{2,1,0:T(8,128)(2,1)} %pot_hbm.1), custom_call_target="tpu_custom_call" | custom-call | tf_op jit(solution)/shard_map/pallas_call | solution.py:350
  26.5 1.2 %shard_map.68 = (bf16[4,16,4096]{2,1,0:T(8,128)(2,1)}, bf16[4,16,4096]{2,1,0:T(8,128)(2,1)}, bf16[4,16,4096]{2,1,0:T(8,128)(2,1)}) custom-call(bf16[4,16,4096]{2,1,0:T(8,128)(2,1)S(1)} %get-tuple-element.6.a, bf16[4,16,4096]{2,1,0:T(8,128)(2,1)S(1)} %get-tuple-element.7.b, bf16[4,16,4096]{2,1,0:T(8,128)(2,1)S(1)} %get-tuple-element.8.c), custom_call_target="tpu_custom_call" | custom-call | tf_op jit(solution)/shard_map/pallas_call | solution.py:388
where the time goes:
time: 27.9 us; the launch traced here: 27.7 us
  Pallas kernels  27.1 us (97%)
  between operations  0.64 us (2%)
    pallas_call x1, Pallas kernels, on_device(): pl.pallas_call(functools.partial(lens_kernel, los, sky, chunks, width), o...  25.8 us
    pallas_call x1, Pallas kernels, on_device(): pl.pallas_call(store_kernel, out_shape=[jax.ShapeDtypeStruct(potentials.s...  1.24 us

commit v1 on v0

v1 whole, which is shorter than its diff:
```python
import functools

import jax
import jax.numpy as jnp
from jax import lax
from jax.experimental import pallas as pl
from jax.experimental.pallas import tpu as pltpu
from jax.sharding import PartitionSpec as P

MESH = pl.DeviceIdType.MESH
WIDTH = 128
TAIL = 6
EDGE_LAG = 6
BACK_LAG = 7


def schedule(n, tail, edge_lag, back_lag):
    mapped = {}
    for c in range(n):
        late = c < n - tail
        mapped[c] = c + (edge_lag if late else 0)
        mapped[n + c] = c + back_lag + (edge_lag if late else 0)
    span = 2 * n
    ready = {c: max(mapped[(c - 1) % span], mapped[c], mapped[(c + 1) % span]) for c in range(span)}
    steps = []
    for i in range(max(ready.values()) + 1):
        events = []
        if i < n:
            events.append(("sum", 0, i >= n - tail))
        if 0 <= i - back_lag < n:
            events.append(("take", n - back_lag, i - back_lag >= n - tail))
        for c in range(span):
            if mapped[c] == i:
                events.append(("lens", c - i, c % n >= n - tail))
        for c in range(span):
            if ready[c] == i:
                events.append(("out", c - i, False))
        steps.append(tuple(events))
    return steps


def lens_kernel(
    los, sky, n, tail, width, weight_hbm, dist_hbm, source_hbm, pot_hbm,
    conv_ref, one_ref, two_ref,
    weight_ref, dist_ref, source_ref, pot, edge_send, edge_recv, sent, own, got,
    onward, before, back, prefix, rim_send, rim_below, rim_above, rim_pot, lens, slopes,
    scalar_sem, load_sem, edge_ssem, edge_rsem, x_ssem, x_rsem, z_ssem, z_rsem, b_ssem, b_rsem,
    up_ssem, up_rsem, down_ssem, down_rsem,
):
    f32, bf16 = jnp.float32, jnp.bfloat16
    shells, rows = pot.shape[0], pot.shape[1]
    main, full, span = 2 * rows, 2 * rows + 8, 2 * n
    me = lax.axis_index("los")
    strip = lax.axis_index("sky")
    q = me // 2
    r = me % 2
    last = los // 2 - 1
    partner = me + 1 - 2 * r
    up = (strip + sky - 1) % sky
    down = (strip + 1) % sky
    mine_at = r * n
    theirs_at = (1 - r) * n

    scalars = [
        pltpu.make_async_copy(src, dst, scalar_sem.at[i])
        for i, (src, dst) in enumerate(
            ((weight_hbm, weight_ref), (dist_hbm, dist_ref), (source_hbm, source_ref))
        )
    ]
    for copy in scalars:
        copy.start()
    groups = load_sem.shape[0] // 2
    wide = n // groups * width
    loads = []
    for g in range(2 * groups):
        part = (1 - r) if g < groups else r
        cols = pl.ds(pl.multiple_of((part * groups + g % groups) * wide, 128), wide)
        loads.append(
            pltpu.make_async_copy(pot_hbm.at[:, :, cols], pot.at[:, :, cols], load_sem.at[g])
        )
        loads[-1].start()

    barrier = pltpu.get_barrier_semaphore()
    pl.semaphore_signal(barrier, inc=1, device_id={"los": partner}, device_id_type=MESH)
    pl.semaphore_signal(barrier, inc=1, device_id={"sky": up}, device_id_type=MESH)
    pl.semaphore_signal(barrier, inc=1, device_id={"sky": down}, device_id_type=MESH)

    @pl.when(q > 0)
    def _():
        pl.semaphore_signal(barrier, inc=1, device_id={"los": me - 2}, device_id_type=MESH)

    @pl.when(q < last)
    def _():
        pl.semaphore_signal(barrier, inc=1, device_id={"los": me + 2}, device_id_type=MESH)

    def columns(b):
        return pl.ds(pl.multiple_of(b * width, 128), width)

    @pl.when(q == 0)
    def _():
        def clear(c, carry):
            before[c] = jnp.zeros((full, width), f32)
            return carry

        lax.fori_loop(0, n, clear, 0)

    for copy in scalars:
        copy.wait()
    scale = 1.0 / 24.0
    near = [weight_ref[j] * dist_ref[j] * scale for j in range(shells)]
    far = [near[j] * dist_ref[j] for j in range(shells)]
    row = lax.broadcasted_iota(jnp.int32, (8, width), 0)
    lane = lax.broadcasted_iota(jnp.int32, (8, width), 1)
    inverse = [1.0 / jnp.full((8, width), source_ref[j], f32) for j in range(shells)]

    def tall(x):
        return jnp.concatenate([x] * (rows // 8), axis=0)

    def totals(b):
        total_near = jnp.zeros((rows, width), f32)
        total_far = jnp.zeros((rows, width), f32)
        for j in range(shells):
            block = pot[j, :, columns(b)].astype(f32)
            total_near = total_near + near[j] * block
            total_far = total_far + far[j] * block
        return total_near, total_far

    def remote(src, dst, ssem, rsem, **where):
        return pltpu.make_async_remote_copy(
            src_ref=src, dst_ref=dst, send_sem=ssem, recv_sem=rsem,
            device_id=where, device_id_type=MESH,
        )

    def part(ref, c, rim):
        return ref.at[c, pl.ds(0, full if rim else main)]

    def x_copy(c, rim):
        return remote(part(sent, c, rim), part(got, c, rim), x_ssem.at[c], x_rsem.at[c], los=partner)

    def z_copy(c, rim):
        return remote(
            part(onward, c, rim), part(before, c, rim), z_ssem.at[c], z_rsem.at[c], los=me + 2
        )

    def b_copy(c, rim):
        return remote(
            part(back, c, rim), part(prefix, mine_at + c, rim), b_ssem.at[c], b_rsem.at[c], los=partner
        )

    def b_arrival(c, rim):
        return remote(
            part(back, c, rim), part(prefix, theirs_at + c, rim), b_ssem.at[c], b_rsem.at[c], los=partner
        )

    def up_copy(b):
        return remote(rim_send.at[b], rim_below.at[b], up_ssem.at[b], up_rsem.at[b], sky=up)

    def down_copy(b):
        return remote(rim_send.at[b], rim_above.at[b], down_ssem.at[b], down_rsem.at[b], sky=down)

    edges = [
        remote(edge_send.at[0], edge_recv.at[0], edge_ssem.at[0], edge_rsem.at[0], sky=up),
        remote(edge_send.at[1], edge_recv.at[1], edge_ssem.at[1], edge_rsem.at[1], sky=down),
    ]

    def fill(ref, c, b):
        total_near, total_far = totals(b)
        ref[c, :rows] = total_near
        ref[c, rows:main] = total_far

    loads[0].wait()
    fill(sent, 0, theirs_at)

    peers = 3 + (q > 0).astype(jnp.int32) + (q < last).astype(jnp.int32)
    pl.semaphore_wait(barrier, peers)
    x_copy(0, n - tail <= 0).start()

    def send_totals(c, carry):
        fill(sent, c, theirs_at + c)
        x_copy(c, False).start()
        return carry

    early = min(n // groups, n - tail)
    lax.fori_loop(1, early, send_totals, 0)
    for copy in loads[1:]:
        copy.wait()

    def pack(b, carry):
        top = jnp.zeros((8, width), f32)
        bottom = jnp.zeros((8, width), f32)
        for j in range(shells):
            block = pot[j, :, columns(b)].astype(f32)
            mine = (row >= 2 * j) & (row < 2 * j + 2)
            top = jnp.where(mine, pltpu.roll(block[:8], (2 * j) % 8, 0), top)
            bottom = jnp.where(mine, pltpu.roll(block[rows - 8 :], (2 * j + 2) % 8, 0), bottom)
        edge_send[0, :, columns(b)] = top.astype(bf16)
        edge_send[1, :, columns(b)] = bottom.astype(bf16)
        return carry

    lax.fori_loop(0, span, pack, 0, unroll=4)
    for copy in edges:
        copy.start()
    lax.fori_loop(early, n - tail, send_totals, 0)

    def tail_totals(c, carry):
        fill(sent, c, theirs_at + c)
        return carry

    lax.fori_loop(n - tail, n, tail_totals, 0)

    def own_totals(c, carry):
        fill(own, c, mine_at + c)
        return carry

    lax.fori_loop(0, n, own_totals, 0, unroll=2)

    for copy in edges:
        copy.wait_recv()

    inner = (row >= 2) & (row < 6)

    def rims(b, total_of):
        below = edge_recv[0, :, columns(b)].astype(f32)
        above = edge_recv[1, :, columns(b)].astype(f32)
        total = jnp.zeros((8, width), f32)
        for j in range(shells):
            tile = jnp.where(
                row < 2,
                pltpu.roll(below, (8 - 2 * j) % 8, 0),
                jnp.where(
                    row < 4,
                    pltpu.roll(below, (10 - 2 * j) % 8, 0),
                    jnp.where(
                        row < 6,
                        pltpu.roll(above, (12 - 2 * j) % 8, 0),
                        pltpu.roll(above, (14 - 2 * j) % 8, 0),
                    ),
                ),
            )
            scaled = tile * jnp.where(inner, far[j], near[j])
            rim_pot[b, j] = scaled
            total = total + scaled
        if total_of is not None:
            ref, c = total_of
            ref[c, main:full] = total

    def tail_rims(c, carry):
        rims(theirs_at + c, (sent, c))
        x_copy(c, True).start()
        return carry

    def own_rims(c, carry):
        rims(mine_at + c, (own, c))
        return carry

    def other_rims(c, carry):
        rims(mine_at + c, None)
        rims(theirs_at + c, None)
        return carry

    lax.fori_loop(n - tail, n, tail_rims, 0)
    lax.fori_loop(n - tail, n, own_rims, 0)
    lax.fori_loop(0, n - tail, other_rims, 0)

    is_odd = r.astype(f32)
    is_even = 1.0 - is_odd

    def send_rim(b, sums):
        first_near, last_near = sums[:8], sums[rows - 8 : rows]
        first_far, last_far = sums[rows : rows + 8], sums[main - 8 : main]
        rim_send[b] = jnp.where(
            row < 2,
            first_near,
            jnp.where(
                row < 4,
                pltpu.roll(first_far, 2, 0),
                jnp.where(row < 6, pltpu.roll(last_far, 6, 0), last_near),
            ),
        )
        up_copy(b).start()
        down_copy(b).start()

    def add_up(c, rim):
        x_copy(c, rim).wait_recv()

        @pl.when(q > 0)
        def _():
            z_copy(c, rim).wait_recv()

        size = full if rim else main
        mine, other, base = own[c, :size], got[c, :size], before[c, :size]
        onward[c, :size] = base + (mine + other)

        @pl.when(q < last)
        def _():
            z_copy(c, rim).start()

        back[c, :size] = base + is_even * mine
        b_copy(c, rim).start()
        kept = base + is_odd * other
        prefix[mine_at + c, :size] = kept
        if not rim:
            send_rim(mine_at + c, kept)

    def take(c, rim):
        b_arrival(c, rim).wait_recv()
        if not rim:
            send_rim(theirs_at + c, prefix[theirs_at + c, :main])

    def map_block(b, rim):
        run_near = prefix[b, :rows]
        run_far = prefix[b, rows:main]
        if rim:
            edge = prefix[b, main:full]
        else:
            up_copy(b).wait_recv()
            down_copy(b).wait_recv()
            edge = jnp.where(row < 4, rim_below[b], rim_above[b])
        for j in range(shells):
            block = pot[j, :, columns(b)].astype(f32)
            run_near = run_near + near[j] * block
            run_far = run_far + far[j] * block
            edge = edge + rim_pot[b, j]
            far_edge = jnp.where(row < 4, pltpu.roll(edge, 6, 0), pltpu.roll(edge, 2, 0))
            border = edge - far_edge * inverse[j]
            lens[b, j, :8] = border
            lens[b, j, 8 : 8 + rows] = run_near - run_far * tall(inverse[j])
            lens[b, j, 8 + rows :] = border

    tile = 8 + rows

    def stack(x, count):
        return jnp.concatenate([x] * count, axis=0)

    lanes = stack(lane, tile // 8)

    def out_block(b):
        left_b = (b + span - 1) % span
        right_b = (b + 1) % span
        cols = columns(b)
        for j in range(shells):
            centre = lens[b, j, :tile]
            left = lens[left_b, j, :tile]
            right = lens[right_b, j, :tile]

            def shift(k):
                if k > 0:
                    joined = jnp.where(lanes >= width - k, left, centre)
                else:
                    joined = jnp.where(lanes < -k, right, centre)
                return pltpu.roll(joined, k % width, 1)

            left1, right1, left2, right2 = shift(1), shift(-1), shift(2), shift(-2)
            slope = (left2 - right2) + 8.0 * (right1 - left1)
            slopes[j, :tile] = slope
            slopes[j, tile:] = slope[:8]
            second_x = (16.0 * (left1 + right1) - (left2 + right2))[8:]

            def rows_at(ref, k):
                return ref[8 + k : 8 + k + rows]

            here = lens.at[b, j]
            second_y = 16.0 * (rows_at(here, -1) + rows_at(here, 1)) - (
                rows_at(here, -2) + rows_at(here, 2)
            )
            tilt = slopes.at[j]
            cross = (rows_at(tilt, -2) - rows_at(tilt, 2)) + 8.0 * (
                rows_at(tilt, 1) - rows_at(tilt, -1)
            )
            conv_ref[j, :, cols] = (second_x + second_y - 60.0 * centre[8:]).astype(bf16)
            one_ref[j, :, cols] = (second_x - second_y).astype(bf16)
            two_ref[j, :, cols] = (cross * (1.0 / 6.0)).astype(bf16)

    def block_at(c):
        half = (c >= n).astype(jnp.int32)
        return ((r + half) % 2) * n + c - half * n

    def run(edge_lag, back_lag):
        steps = schedule(n, tail, edge_lag, back_lag)
        start = 0
        while start < len(steps):
            stop = start + 1
            while stop < len(steps) and steps[stop] == steps[start]:
                stop += 1

            def body(i, carry, events=steps[start]):
                for event, offset, rim in events:
                    c = i + offset
                    if event == "sum":
                        add_up(c, rim)
                    elif event == "take":
                        take(c - n, rim)
                    elif event == "lens":
                        map_block(block_at(c), rim)
                    else:
                        out_block(block_at(c))
                return carry

            lax.fori_loop(start, stop, body, 0)
            start = stop

    @pl.when(q < 2)
    def _():
        run(EDGE_LAG, n)

    @pl.when(q >= 2)
    def _():
        run(EDGE_LAG, BACK_LAG)

    for copy in edges:
        copy.wait_send()

    def finish(rim):
        def body(c, carry):
            x_copy(c, rim).wait_send()
            b_copy(c, rim).wait_send()

            @pl.when(q < last)
            def _():
                z_copy(c, rim).wait_send()

            if not rim:
                for b in (c, n + c):
                    up_copy(b).wait_send()
                    down_copy(b).wait_send()
            return carry

        return body

    lax.fori_loop(0, n - tail, finish(False), 0)
    lax.fori_loop(n - tail, n, finish(True), 0)


def store_kernel(a, b, c, to_a, to_b, to_c, sems):
    copies = [
        pltpu.make_async_copy(src.at[j], dst.at[j], sems.at[m, j])
        for m, (src, dst) in enumerate(((a, to_a), (b, to_b), (c, to_c)))
        for j in range(a.shape[0])
    ]
    for copy in copies:
        copy.start()
    for copy in copies:
        copy.wait()


def on_device(los, sky, potentials, shell_weight, shell_dist, source_dist):
    shells, rows, ncols = potentials.shape
    width = WIDTH
    n = ncols // 2 // width
    tail = min(n, TAIL)
    groups = next(g for g in (4, 2, 1) if n % g == 0)
    f32, bf16 = jnp.float32, jnp.bfloat16
    dma = pltpu.SemaphoreType.DMA
    vmem = pl.BlockSpec(memory_space=pltpu.VMEM)
    anywhere = pl.BlockSpec(memory_space=pl.ANY)
    full = 2 * rows + 8
    message = pltpu.VMEM((n, full, width), f32)
    small = pltpu.VMEM((2 * n, 8, width), f32)
    scalar = pltpu.SMEM((shells,), f32)
    staged = pl.pallas_call(
        functools.partial(lens_kernel, los, sky, n, tail, width),
        out_shape=[pltpu.VMEM(potentials.shape, bf16)] * 3,
        in_specs=[anywhere] * 4,
        out_specs=[vmem] * 3,
        scratch_shapes=[
            scalar, scalar, scalar,
            pltpu.VMEM(potentials.shape, bf16),
            pltpu.VMEM((2, 8, ncols), bf16),
            pltpu.VMEM((2, 8, ncols), bf16),
            message, message, message, message, message, message,
            pltpu.VMEM((2 * n, full, width), f32),
            small, small, small,
            pltpu.VMEM((2 * n, shells, 8, width), f32),
            pltpu.VMEM((2 * n, shells, rows + 16, width), f32),
            pltpu.VMEM((shells, rows + 16, width), f32),
            dma((3,)), dma((2 * groups,)), dma((2,)), dma((2,)),
            dma((n,)), dma((n,)), dma((n,)), dma((n,)), dma((n,)), dma((n,)),
            dma((2 * n,)), dma((2 * n,)), dma((2 * n,)), dma((2 * n,)),
        ],
        compiler_params=pltpu.CompilerParams(collective_id=0, has_side_effects=True),
    )(shell_weight, shell_dist, source_dist, potentials)
    return tuple(pl.pallas_call(
        store_kernel,
        out_shape=[jax.ShapeDtypeStruct(potentials.shape, bf16)] * 3,
        in_specs=[vmem] * 3,
        out_specs=[anywhere] * 3,
        scratch_shapes=[dma((3, shells))],
    )(*[pltpu.with_memory_space_constraint(x, pltpu.VMEM) for x in staged]))


def solution(mesh):
    return jax.shard_map(
        functools.partial(on_device, mesh.shape["los"], mesh.shape["sky"]),
        mesh=mesh,
        in_specs=(P("los", "sky", None), P("los"), P("los"), P("los")),
        out_specs=(P("los", "sky", None), P("los", "sky", None), P("los", "sky", None)),
        check_vma=False,
    )
```

time: 27.9 us -> 26.5 us (0.950)
  the two profiles are of different devices: /device:TPU:24 before, /device:TPU:25 now
where the time goes in v1:
time: 26.5 us; the launch traced here: 26.3 us
  Pallas kernels  25.7 us (97%)
  between operations  0.64 us (2%)
    pallas_call x1, Pallas kernels, on_device(): pl.pallas_call(functools.partial(lens_kernel, los, sky, n, tail, width),...  24.4 us
    pallas_call x1, Pallas kernels, on_device(): pl.pallas_call(store_kernel, out_shape=[jax.ShapeDtypeStruct(potentials.s...  1.24 us

profile of v1, /device:TPU:25, one launch (start us, length us, event | category | flops | bytes accessed | tf_op | source)
XLA Modules:
  0.0 26.3 jit_solution(5680743878974686763)
XLA Ops:
  0.6 24.4 %shard_map.67 = (bf16[4,16,4096]{2,1,0:T(8,128)(2,1)S(1)}, bf16[4,16,4096]{2,1,0:T(8,128)(2,1)S(1)}, bf16[4,16,4096]{2,1,0:T(8,128)(2,1)S(1)}) custom-call(f32[4]{0:T(128)} %weight_hbm.1, f32[4]{0:T(128)} %dist_hbm.1, f32[4]{0:T(128)} %source_hbm.1, bf16[4,16,4096]{2,1,0:T(8,128)(2,1)} %pot_hbm.1), custom_call_target="tpu_custom_call" | custom-call | tf_op jit(solution)/shard_map/pallas_call | solution.py:460
  25.1 1.2 %shard_map.68 = (bf16[4,16,4096]{2,1,0:T(8,128)(2,1)}, bf16[4,16,4096]{2,1,0:T(8,128)(2,1)}, bf16[4,16,4096]{2,1,0:T(8,128)(2,1)}) custom-call(bf16[4,16,4096]{2,1,0:T(8,128)(2,1)S(1)} %get-tuple-element.6.a, bf16[4,16,4096]{2,1,0:T(8,128)(2,1)S(1)} %get-tuple-element.7.b, bf16[4,16,4096]{2,1,0:T(8,128)(2,1)S(1)} %get-tuple-element.8.c), custom_call_target="tpu_custom_call" | custom-call | tf_op jit(solution)/shard_map/pallas_call | solution.py:482

commit v2 on v1

--- a/solution.py
+++ b/solution.py
@@ -9,7 +9,7 @@
 
 MESH = pl.DeviceIdType.MESH
 WIDTH = 128
-TAIL = 6
+TAIL = 8
 EDGE_LAG = 6
 BACK_LAG = 7
 
@@ -42,10 +42,9 @@
 def lens_kernel(
     los, sky, n, tail, width, weight_hbm, dist_hbm, source_hbm, pot_hbm,
     conv_ref, one_ref, two_ref,
-    weight_ref, dist_ref, source_ref, pot, edge_send, edge_recv, sent, own, got,
-    onward, before, back, prefix, rim_send, rim_below, rim_above, rim_pot, lens, slopes,
-    scalar_sem, load_sem, edge_ssem, edge_rsem, x_ssem, x_rsem, z_ssem, z_rsem, b_ssem, b_rsem,
-    up_ssem, up_rsem, down_ssem, down_rsem,
+    scalar_ref, pot, edge_send, edge_recv, sent, own, inbox,
+    onward, back, prefix, rim_send, rim_recv, rim_pot, lens, slopes,
+    scalar_sem, load_sem, edge_sems, send_sems, sum_rsem, b_rsem, rim_rsem,
 ):
     f32, bf16 = jnp.float32, jnp.bfloat16
     shells, rows = pot.shape[0], pot.shape[1]
@@ -61,24 +60,19 @@
     mine_at = r * n
     theirs_at = (1 - r) * n
 
-    scalars = [
-        pltpu.make_async_copy(src, dst, scalar_sem.at[i])
-        for i, (src, dst) in enumerate(
-            ((weight_hbm, weight_ref), (dist_hbm, dist_ref), (source_hbm, source_ref))
-        )
-    ]
-    for copy in scalars:
-        copy.start()
-    groups = load_sem.shape[0] // 2
-    wide = n // groups * width
+    for i, src in enumerate((weight_hbm, dist_hbm, source_hbm)):
+        pltpu.make_async_copy(src, scalar_ref.at[i], scalar_sem.at[0]).start()
+    first = max(1, n // 4)
     loads = []
-    for g in range(2 * groups):
-        part = (1 - r) if g < groups else r
-        cols = pl.ds(pl.multiple_of((part * groups + g % groups) * wide, 128), wide)
-        loads.append(
-            pltpu.make_async_copy(pot_hbm.at[:, :, cols], pot.at[:, :, cols], load_sem.at[g])
-        )
-        loads[-1].start()
+    for g, (at, count) in enumerate(
+        ((theirs_at, first), (theirs_at + first, n - first), (mine_at, n))
+    ):
+        if count > 0:
+            cols = pl.ds(pl.multiple_of(at * width, 128), count * width)
+            loads.append(
+                pltpu.make_async_copy(pot_hbm.at[:, :, cols], pot.at[:, :, cols], load_sem.at[g])
+            )
+            loads[-1].start()
 
     barrier = pltpu.get_barrier_semaphore()
     pl.semaphore_signal(barrier, inc=1, device_id={"los": partner}, device_id_type=MESH)
@@ -99,19 +93,19 @@
     @pl.when(q == 0)
     def _():
         def clear(c, carry):
-            before[c] = jnp.zeros((full, width), f32)
+            base = pl.multiple_of(c * 8, 8)
+            inbox[1, pl.ds(base, 8)] = jnp.zeros((8, width), f32)
             return carry
 
-        lax.fori_loop(0, n, clear, 0)
-
-    for copy in scalars:
-        copy.wait()
+        lax.fori_loop(0, inbox.shape[1] // 8, clear, 0, unroll=8)
+
+    pltpu.make_async_copy(scalar_ref, scalar_ref, scalar_sem.at[0]).wait()
     scale = 1.0 / 24.0
-    near = [weight_ref[j] * dist_ref[j] * scale for j in range(shells)]
-    far = [near[j] * dist_ref[j] for j in range(shells)]
+    near = [scalar_ref[0, j] * scalar_ref[1, j] * scale for j in range(shells)]
+    far = [near[j] * scalar_ref[1, j] for j in range(shells)]
     row = lax.broadcasted_iota(jnp.int32, (8, width), 0)
     lane = lax.broadcasted_iota(jnp.int32, (8, width), 1)
-    inverse = [1.0 / jnp.full((8, width), source_ref[j], f32) for j in range(shells)]
+    inverse = [1.0 / jnp.full((8, width), scalar_ref[2, j], f32) for j in range(shells)]
 
     def tall(x):
         return jnp.concatenate([x] * (rows // 8), axis=0)
@@ -131,56 +125,66 @@
             device_id=where, device_id_type=MESH,
         )
 
-    def part(ref, c, rim):
-        return ref.at[c, pl.ds(0, full if rim else main)]
+    def at(c, rim):
+        start = c * main + ((c - (n - tail)) * 8 if rim else 0)
+        return pl.ds(pl.multiple_of(start, 8), full if rim else main)
 
     def x_copy(c, rim):
-        return remote(part(sent, c, rim), part(got, c, rim), x_ssem.at[c], x_rsem.at[c], los=partner)
+        rows_of = at(c, rim)
+        return remote(
+            sent.at[rows_of], inbox.at[0, rows_of], send_sems.at[0], sum_rsem.at[c], los=partner
+        )
 
     def z_copy(c, rim):
+        rows_of = at(c, rim)
         return remote(
-            part(onward, c, rim), part(before, c, rim), z_ssem.at[c], z_rsem.at[c], los=me + 2
+            onward.at[rows_of], inbox.at[1, rows_of], send_sems.at[1], sum_rsem.at[c], los=me + 2
         )
 
     def b_copy(c, rim):
+        rows_of = at(c, rim)
         return remote(
-            part(back, c, rim), part(prefix, mine_at + c, rim), b_ssem.at[c], b_rsem.at[c], los=partner
-        )
-
-    def b_arrival(c, rim):
-        return remote(
-            part(back, c, rim), part(prefix, theirs_at + c, rim), b_ssem.at[c], b_rsem.at[c], los=partner
-        )
-
-    def up_copy(b):
-        return remote(rim_send.at[b], rim_below.at[b], up_ssem.at[b], up_rsem.at[b], sky=up)
-
-    def down_copy(b):
-        return remote(rim_send.at[b], rim_above.at[b], down_ssem.at[b], down_rsem.at[b], sky=down)
+            back.at[rows_of], prefix.at[r, rows_of], send_sems.at[2], b_rsem.at[c], los=partner
+        )
+
+    def arrived(ref, sem):
+        pltpu.make_async_copy(ref, ref, sem).wait()
+
+    def slot(b):
+        return b - (b // n) * tail
+
+    def rim_copies(b):
+        src, dst, sem = rim_send.at[slot(b)], rim_recv.at[slot(b)], rim_rsem.at[slot(b)]
+        return (
+            remote(src, dst.at[0], send_sems.at[3], sem, sky=up),
+            remote(src, dst.at[1], send_sems.at[3], sem, sky=down),
+        )
 
     edges = [
-        remote(edge_send.at[0], edge_recv.at[0], edge_ssem.at[0], edge_rsem.at[0], sky=up),
-        remote(edge_send.at[1], edge_recv.at[1], edge_ssem.at[1], edge_rsem.at[1], sky=down),
+        remote(edge_send.at[0], edge_recv.at[0], edge_sems.at[0], edge_sems.at[1], sky=up),
+        remote(edge_send.at[1], edge_recv.at[1], edge_sems.at[0], edge_sems.at[1], sky=down),
     ]
 
-    def fill(ref, c, b):
+    def fill(ref, c, b, rim=False):
         total_near, total_far = totals(b)
-        ref[c, :rows] = total_near
-        ref[c, rows:main] = total_far
+        start = at(c, rim).start
+        ref[pl.ds(start, rows)] = total_near
+        ref[pl.ds(start + rows, rows)] = total_far
 
     loads[0].wait()
-    fill(sent, 0, theirs_at)
+    fill(sent, 0, theirs_at, n == tail)
 
     peers = 3 + (q > 0).astype(jnp.int32) + (q < last).astype(jnp.int32)
     pl.semaphore_wait(barrier, peers)
-    x_copy(0, n - tail <= 0).start()
+    if n > tail:
+        x_copy(0, False).start()
 
     def send_totals(c, carry):
         fill(sent, c, theirs_at + c)
         x_copy(c, False).start()
         return carry
 
-    early = min(n // groups, n - tail)
+    early = min(first, n - tail)
     lax.fori_loop(1, early, send_totals, 0)
     for copy in loads[1:]:
         copy.wait()
@@ -200,10 +204,11 @@
     lax.fori_loop(0, span, pack, 0, unroll=4)
     for copy in edges:
         copy.start()
-    lax.fori_loop(early, n - tail, send_totals, 0)
+    lax.fori_loop(max(1, early), n - tail, send_totals, 0)
 
     def tail_totals(c, carry):
-        fill(sent, c, theirs_at + c)
+        fill(sent, c, theirs_at + c, True)
+        fill(own, c, mine_at + c, True)
         return carry
 
     lax.fori_loop(n - tail, n, tail_totals, 0)
@@ -212,10 +217,9 @@
         fill(own, c, mine_at + c)
         return carry
 
-    lax.fori_loop(0, n, own_totals, 0, unroll=2)
-
-    for copy in edges:
-        copy.wait_recv()
+    lax.fori_loop(0, n - tail, own_totals, 0)
+
+    arrived(edge_recv, edge_sems.at[1])
 
     inner = (row >= 2) & (row < 6)
 
@@ -242,7 +246,7 @@
             total = total + scaled
         if total_of is not None:
             ref, c = total_of
-            ref[c, main:full] = total
+            ref[pl.ds(at(c, True).start + main, 8)] = total
 
     def tail_rims(c, carry):
         rims(theirs_at + c, (sent, c))
@@ -268,7 +272,7 @@
     def send_rim(b, sums):
         first_near, last_near = sums[:8], sums[rows - 8 : rows]
         first_far, last_far = sums[rows : rows + 8], sums[main - 8 : main]
-        rim_send[b] = jnp.where(
+        rim_send[slot(b)] = jnp.where(
             row < 2,
             first_near,
             jnp.where(
@@ -277,45 +281,51 @@
                 jnp.where(row < 6, pltpu.roll(last_far, 6, 0), last_near),
             ),
         )
-        up_copy(b).start()
-        down_copy(b).start()
+        for copy in rim_copies(b):
+            copy.start()
 
     def add_up(c, rim):
-        x_copy(c, rim).wait_recv()
+        rows_of = at(c, rim)
+
+        @pl.when(q == 0)
+        def _():
+            arrived(inbox.at[0, rows_of], sum_rsem.at[c])
 
         @pl.when(q > 0)
         def _():
-            z_copy(c, rim).wait_recv()
-
-        size = full if rim else main
-        mine, other, base = own[c, :size], got[c, :size], before[c, :size]
-        onward[c, :size] = base + (mine + other)
+            arrived(inbox.at[:, rows_of], sum_rsem.at[c])
+
+        mine, other, base = own[rows_of], inbox[0, rows_of], inbox[1, rows_of]
+        onward[rows_of] = base + (mine + other)
 
         @pl.when(q < last)
         def _():
             z_copy(c, rim).start()
 
-        back[c, :size] = base + is_even * mine
+        back[rows_of] = base + is_even * mine
         b_copy(c, rim).start()
         kept = base + is_odd * other
-        prefix[mine_at + c, :size] = kept
+        prefix[r, rows_of] = kept
         if not rim:
             send_rim(mine_at + c, kept)
 
     def take(c, rim):
-        b_arrival(c, rim).wait_recv()
+        rows_of = at(c, rim)
+        arrived(prefix.at[1 - r, rows_of], b_rsem.at[c])
         if not rim:
-            send_rim(theirs_at + c, prefix[theirs_at + c, :main])
+            send_rim(theirs_at + c, prefix[1 - r, rows_of])
 
     def map_block(b, rim):
-        run_near = prefix[b, :rows]
-        run_far = prefix[b, rows:main]
+        half = b // n
+        c = b - half * n
+        sums = prefix[half, at(c, rim)]
+        run_near = sums[:rows]
+        run_far = sums[rows:main]
         if rim:
-            edge = prefix[b, main:full]
+            edge = sums[main:]
         else:
-            up_copy(b).wait_recv()
-            down_copy(b).wait_recv()
-            edge = jnp.where(row < 4, rim_below[b], rim_above[b])
+            arrived(rim_recv.at[slot(b)], rim_rsem.at[slot(b)])
+            edge = jnp.where(row < 4, rim_recv[slot(b), 0], rim_recv[slot(b), 1])
         for j in range(shells):
             block = pot[j, :, columns(b)].astype(f32)
             run_near = run_near + near[j] * block
@@ -407,28 +417,15 @@
     def _():
         run(EDGE_LAG, BACK_LAG)
 
-    for copy in edges:
-        copy.wait_send()
-
-    def finish(rim):
-        def body(c, carry):
-            x_copy(c, rim).wait_send()
-            b_copy(c, rim).wait_send()
-
-            @pl.when(q < last)
-            def _():
-                z_copy(c, rim).wait_send()
-
-            if not rim:
-                for b in (c, n + c):
-                    up_copy(b).wait_send()
-                    down_copy(b).wait_send()
-            return carry
-
-        return body
-
-    lax.fori_loop(0, n - tail, finish(False), 0)
-    lax.fori_loop(n - tail, n, finish(True), 0)
+    arrived(edge_send, edge_sems.at[0])
+    arrived(sent, send_sems.at[0])
+    arrived(back, send_sems.at[2])
+    if n > tail:
+        arrived(rim_recv, send_sems.at[3])
+
+    @pl.when(q < last)
+    def _():
+        arrived(onward, send_sems.at[1])
 
 
 def store_kernel(a, b, c, to_a, to_b, to_c, sems):
@@ -448,34 +445,31 @@
     width = WIDTH
     n = ncols // 2 // width
     tail = min(n, TAIL)
-    groups = next(g for g in (4, 2, 1) if n % g == 0)
     f32, bf16 = jnp.float32, jnp.bfloat16
     dma = pltpu.SemaphoreType.DMA
     vmem = pl.BlockSpec(memory_space=pltpu.VMEM)
     anywhere = pl.BlockSpec(memory_space=pl.ANY)
-    full = 2 * rows + 8
-    message = pltpu.VMEM((n, full, width), f32)
-    small = pltpu.VMEM((2 * n, 8, width), f32)
-    scalar = pltpu.SMEM((shells,), f32)
+    lines = n * 2 * rows + tail * 8
+    message = pltpu.VMEM((lines, width), f32)
+    pair = pltpu.VMEM((2, lines, width), f32)
+    slots = max(1, 2 * (n - tail))
     staged = pl.pallas_call(
         functools.partial(lens_kernel, los, sky, n, tail, width),
         out_shape=[pltpu.VMEM(potentials.shape, bf16)] * 3,
         in_specs=[anywhere] * 4,
         out_specs=[vmem] * 3,
         scratch_shapes=[
-            scalar, scalar, scalar,
+            pltpu.SMEM((3, shells), f32),
             pltpu.VMEM(potentials.shape, bf16),
             pltpu.VMEM((2, 8, ncols), bf16),
             pltpu.VMEM((2, 8, ncols), bf16),
-            message, message, message, message, message, message,
-            pltpu.VMEM((2 * n, full, width), f32),
-            small, small, small,
+            message, message, pair, message, message, pair,
+            pltpu.VMEM((slots, 8, width), f32),
+            pltpu.VMEM((slots, 2, 8, width), f32),
             pltpu.VMEM((2 * n, shells, 8, width), f32),
             pltpu.VMEM((2 * n, shells, rows + 16, width), f32),
             pltpu.VMEM((shells, rows + 16, width), f32),
-            dma((3,)), dma((2 * groups,)), dma((2,)), dma((2,)),
-            dma((n,)), dma((n,)), dma((n,)), dma((n,)), dma((n,)), dma((n,)),
-            dma((2 * n,)), dma((2 * n,)), dma((2 * n,)), dma((2 * n,)),
+            dma((1,)), dma((3,)), dma((2,)), dma((4,)), dma((n,)), dma((n,)), dma((slots,)),
         ],
         compiler_params=pltpu.CompilerParams(collective_id=0, has_side_effects=True),
     )(shell_weight, shell_dist, source_dist, potentials)

time: 26.5 us -> 24.4 us (0.921)
  Pallas kernels: 25.7 us -> 23.6 us
    pallas_call x1, Pallas kernels: 24.4 us -> 22.4 us  [on_device(): pl.pallas_call(functools.partial(lens_kernel, los, sky, n, tail, width),...]
where the time goes in v2:
time: 24.4 us; the launch traced here: 24.3 us
  Pallas kernels  23.6 us (97%)
  between operations  0.64 us (3%)
    pallas_call x1, Pallas kernels, on_device(): pl.pallas_call(functools.partial(lens_kernel, los, sky, n, tail, width),...  22.4 us
    pallas_call x1, Pallas kernels, on_device(): pl.pallas_call(store_kernel, out_shape=[jax.ShapeDtypeStruct(potentials.s...  1.24 us

profile of v2, /device:TPU:25, one launch (start us, length us, event | category | flops | bytes accessed | tf_op | source)
XLA Modules:
  0.0 24.3 jit_solution(8145879935685453060)
XLA Ops:
  0.6 22.4 %shard_map.67 = (bf16[4,16,4096]{2,1,0:T(8,128)(2,1)S(1)}, bf16[4,16,4096]{2,1,0:T(8,128)(2,1)S(1)}, bf16[4,16,4096]{2,1,0:T(8,128)(2,1)S(1)}) custom-call(f32[4]{0:T(128)} %weight_hbm.1, f32[4]{0:T(128)} %dist_hbm.1, f32[4]{0:T(128)} %source_hbm.1, bf16[4,16,4096]{2,1,0:T(8,128)(2,1)} %pot_hbm.1), custom_call_target="tpu_custom_call" | custom-call | tf_op jit(solution)/shard_map/pallas_call | solution.py:456
  23.0 1.2 %shard_map.68 = (bf16[4,16,4096]{2,1,0:T(8,128)(2,1)}, bf16[4,16,4096]{2,1,0:T(8,128)(2,1)}, bf16[4,16,4096]{2,1,0:T(8,128)(2,1)}) custom-call(bf16[4,16,4096]{2,1,0:T(8,128)(2,1)S(1)} %get-tuple-element.6.a, bf16[4,16,4096]{2,1,0:T(8,128)(2,1)S(1)} %get-tuple-element.7.b, bf16[4,16,4096]{2,1,0:T(8,128)(2,1)S(1)} %get-tuple-element.8.c), custom_call_target="tpu_custom_call" | custom-call | tf_op jit(solution)/shard_map/pallas_call | solution.py:476
